TPU v7x, 32 devices: a whole 2x2x4 slice. The times are simulated.
32 devices in a mesh: row: 8 (over z, x), ba: 4 (over y, core).
Axes of the slice: x: 2, y: 2, z: 4, core: 2. Of those that a mesh axis runs over, the one named last changes fastest.
Arguments:
- constants: float32 [8, 192, 36864], P('row', 'ba'), may hold values from -6 to 6
- current_modes: float32 [8, 2, 192, 4], P('row', None, 'ba'), may hold values from -0.4375 to 0.4375
- owner_id: int32 [1], replicated, may hold values from 0 to 7
- live_count: int32 [8], P('row'), may hold values from 0 to 1, as said below
- triplets: int32 [8, 6], P('row'), may hold values from -3 to 3
- center_point: int32 [3], replicated, may hold values from 0 to 31
- pair_points: int32 [64, 3], P('row'), may hold values from 0 to 31
- first_vectors: float32 [64, 2, 36864], P('row'), may hold values from -0.4375 to 0.4375
- second_vectors: float32 [64, 2, 36864], P('row'), may hold values from -0.4375 to 0.4375
Outputs:
- strength: float32 [64, 4, 36864], P('row', 'ba')
Inputs may be any that keep to these rules, and one draw needn't show every extreme that they name: Shard j uses its first live_count[j] slots; the constants and triplets of the other slots are ignored. A shard may use none. Some shard uses all 1 slots.
All inputs are finite; a program needn't handle non-finite values.
Results may differ from a plain program's by a relative error of at most 0.00008.
Values sent between devices are 32-bit elements; how exact they have to be, the bound alone decides.
No kernel may reach another device: no remote copies, remote signals or barrier semaphores. Data moves between devices by JAX's collectives and lax.ppermute only.
A program may use at most 128 MiB of HBM per device.

v0:
```python
import math
import jax
import jax.numpy as jnp
from jax import lax
from jax.sharding import PartitionSpec as P

B = 192
G = 32
HIGHEST = lax.Precision.HIGHEST
FULL_TURN = 2.0 * math.pi


def broadcast(shard, axis, root):
    mine = lax.axis_index(axis) == root
    return lax.psum(jnp.where(mine, shard, jnp.zeros_like(shard)), axis)


def rotation_table(pair_rows, shift_rows, grid_size):
    turns = (
        jnp.sum(pair_rows[:, :, None] * shift_rows[None, 0:3, :], axis=1) - shift_rows[3][None, :]
    )
    angle = jnp.mod(turns, grid_size).astype(jnp.float32) * (FULL_TURN / grid_size)
    cosine = jnp.cos(angle)
    sine = jnp.sin(angle)
    upper_row = jnp.stack([cosine, -sine], axis=1)
    lower_row = jnp.stack([sine, cosine], axis=1)
    return jnp.stack([upper_row, lower_row], axis=1)


def complex_block(vectors, branches):
    pair_count = vectors.shape[0]
    real_part = vectors[:, 0].reshape(pair_count, branches, branches)
    imag_part = vectors[:, 1].reshape(pair_count, branches, branches)
    upper_row = jnp.stack([real_part, -imag_part], axis=1)
    lower_row = jnp.stack([imag_part, real_part], axis=1)
    return jnp.stack([upper_row, lower_row], axis=1)


def strengths(phase_sum, first_vectors, second_vectors, branches, total_slots):
    pair_count = phase_sum.shape[0]
    band_count = phase_sum.shape[1]
    shaped = phase_sum.reshape(pair_count, band_count, 2, branches, branches)
    partial_sum = jnp.einsum(
        "knibc,koicm->knobm", shaped, complex_block(second_vectors, branches), precision=HIGHEST
    )
    amplitude = jnp.einsum(
        "kojbp,knjbm->knopm", complex_block(first_vectors, branches), partial_sum, precision=HIGHEST
    )
    result = (
        amplitude[:, :, 0] * amplitude[:, :, 0] + amplitude[:, :, 1] * amplitude[:, :, 1]
    ) / total_slots
    return result.reshape(pair_count, band_count, branches * branches)


def body(
    constants,
    current_modes,
    owner_id,
    live_count,
    triplets,
    center_point,
    pair_points,
    first_vectors,
    second_vectors,
):
    slot_count = constants.shape[0]
    eigen = broadcast(current_modes[0], "row", owner_id[0])
    weight = (jnp.arange(slot_count, dtype=jnp.int32) < live_count[0]).astype(jnp.float32)
    term = jnp.einsum("san,rax->nsrx", eigen, constants, precision=HIGHEST)
    contracted = lax.psum_scatter(
        term * weight[None, None, :, None], "ba", scatter_dimension=0, tiled=True
    )
    second_cell = triplets[:, 3:6]
    offsets = triplets[:, 0:3] - second_cell
    point_shift = jnp.sum(second_cell * center_point[None, :], axis=1)
    shift_rows = jnp.concatenate([offsets.T, point_shift[None, :]], axis=0)
    geometry = shift_rows.astype(jnp.float32)[None]
    shard_block = lax.all_gather(contracted, "row", axis=2, tiled=True)
    shard_geometry = lax.all_gather(geometry, "row", axis=2, tiled=True)
    rotation = rotation_table(pair_points, shard_geometry[0].astype(jnp.int32), G)
    phase_sum = jnp.einsum("kuir,nirx->knux", rotation, shard_block, precision=HIGHEST)
    total_slots = slot_count * lax.axis_size("row")
    return strengths(phase_sum, first_vectors, second_vectors, B, total_slots)


def solution(mesh):
    return jax.shard_map(
        body,
        mesh=mesh,
        in_specs=(
            P("row", "ba", None),
            P("row", None, "ba", None),
            P(),
            P("row"),
            P("row", None),
            P(),
            P("row", None),
            P("row", None, None),
            P("row", None, None),
        ),
        out_specs=P("row", "ba", None),
        check_vma=False,
    )
```

profile of v0, /device:TPU:0, one launch (start us, length us, event | category | flops | bytes accessed | tf_op | source)
XLA Modules:
  0.0 172.8 jit_solution(9790825967752891447)
XLA Ops:
  7.2 23.1 %psum.7 = f32[2,48,4]{1,2,0:T(4,128)S(1)} all-reduce(f32[2,48,4]{1,2,0:T(4,128)S(1)} %select_bitcast_fusion), channel_id=1, replica_groups=mesh['row'=8,'ba'=4] {'row'}, use_global_device_ids=true, to_apply=%region_0.1 | all-reduce | flops 384 | bytes 3072 | tf_op jit(solution)/shard_map/psum | solution.py:15
  31.0 5.8 %fusion = f32[4,2,1,36864]{3,0,1,2:T(4,128)S(1)} fusion(f32[2,48,4]{1,2,0:T(4,128)S(1)} %psum.7, f32[1,48,36864]{2,1,0:T(8,128)} %param.9, f32[]{:T(128)} %bitcast.6), kind=kOutput, calls=%fused_computation.2 | convolution fusion | flops 170164224 | bytes 8259076 | tf_op jit(solution)/shard_map/san,rax->nsrx/dot_general | solution.py:69
  36.9 1.9 %copy.51 = f32[4,2,1,36864]{3,1,2,0:T(2,128)} copy(f32[4,2,1,36864]{3,0,1,2:T(4,128)S(1)} %fusion) | data formatting | bytes 2359296 | tf_op jit(solution)/shard_map/mul | solution.py:71
  39.5 34.3 %all-reduce.3.cloned.1.call-done = f32[4,2,1,36864]{3,1,2,0:T(2,128)} async-done(((f32[4,2,1,36864]{3,1,2,0:T(2,128)}), f32[4,2,1,36864]{3,1,2,0:T(2,128)}) %all-reduce.3.cloned.1.call-update) | async-done | bytes 1179664
  73.8 2.3 %dynamic-slice_bitcast_fusion = f32[1,2,1,36864]{3,1,0,2:T(2,128)} fusion(f32[4,2,1,36864]{3,1,2,0:T(2,128)} %all-reduce.3.cloned.1.call-done, u32[]{:T(128)} %bitcast.46), kind=kLoop, calls=%fused_computation.29 | loop fusion | bytes 589828 | tf_op jit(solution)/shard_map/reduce_scatter | solution.py:70
  76.2 0.7 subtract_bitcast_fusion
  76.9 0.7 fusion.29
  77.6 21.0 %all_gather.7 = f32[1,4,8]{1,0,2:T(1,128)S(1)} all-gather(f32[1,4,1]{1,0,2:T(1,128)S(1)} %fusion.29), channel_id=1, replica_groups=mesh['row'=8,'ba'=4] {'row'}, dimensions={2}, use_global_device_ids=true | all-gather | bytes 144 | tf_op jit(solution)/shard_map/all_gather | solution.py:79
  98.7 7.2 %slice_reduce_fusion.2 = (f32[8,36864]{1,0:T(8,128)S(1)}, f32[8,36864]{1,0:T(8,128)}) fusion(f32[8,2,36864]{2,1,0:T(2,128)S(1)} %copy-done.3), kind=kLoop, calls=%fused_computation.27 | loop fusion | bytes 4718592 | tf_op jit(solution)/shard_map/slice | solution.py:33
  105.9 0.7 reshape_squeeze.6
  107.2 1.3 neg.30
  108.5 2.0 %stack_reshape_squeeze.4 = f32[8,1,192,192]{3,2,0,1:T(8,128)S(1)} reshape(f32[8,36864]{1,0:T(8,128)} %get-tuple-element.6) | data formatting | bytes 2359296 | tf_op jit(solution)/shard_map/stack;reshape;squeeze | solution.py:34
  110.5 1.8 %copy.48 = f32[8,1,192,192]{2,3,1,0:T(8,128)} copy(f32[8,1,192,192]{3,2,0,1:T(8,128)S(1)} %stack_reshape_squeeze.4) | data formatting | bytes 2359296 | tf_op jit(solution)/shard_map/stack;reshape;squeeze | solution.py:34
  112.3 10.4 %slice_reduce_fusion = (f32[8,36864]{1,0:T(8,128)}, f32[8,36864]{1,0:T(8,128)}) fusion(f32[8,2,36864]{2,1,0:T(2,128)} %param.16), kind=kLoop, calls=%fused_computation.25 | loop fusion | bytes 4718592 | tf_op jit(solution)/shard_map/slice | solution.py:33
  122.7 2.0 %reshape_squeeze.7 = f32[8,1,192,192]{3,2,0,1:T(8,128)S(1)} reshape(f32[8,36864]{1,0:T(8,128)} %get-tuple-element.7) | data formatting | bytes 2359296 | tf_op jit(solution)/shard_map/reshape;squeeze | solution.py:33
  124.7 3.2 %stack_reshape_squeeze.5 = f32[8,1,192,192]{3,2,0,1:T(8,128)} reshape(f32[8,36864]{1,0:T(8,128)} %get-tuple-element.8) | data formatting | bytes 2359296 | tf_op jit(solution)/shard_map/stack;reshape;squeeze | solution.py:34
  128.3 5.7 %maximum_bitcast_fusion = (f32[8,1,2,192,192]{3,4,2,1,0:T(8,128)}, f32[8,1,2,192,192]{3,4,2,1,0:T(8,128)}) fusion(f32[8,1,192,192]{2,3,1,0:T(8,128)} %neg.30, f32[8,1,192,192]{2,3,1,0:T(8,128)} %copy.48, f32[8,1,192,192]{2,3,1,0:T(8,128)S(1)} %copy.47), kind=kLoop, calls=%fused_computation.12 | loop fusion | flops 1179648 | bytes 8257536 | tf_op jit(solution)/shard_map/stack | solution.py:36
  134.1 1.3 copy-done.2
  135.4 3.5 %maximum_bitcast_fusion.2 = (f32[8,1,2,192,192]{4,3,2,1,0:T(8,128)}, f32[8,1,2,192,192]{4,3,2,1,0:T(8,128)}) fusion(f32[8,1,192,192]{3,2,1,0:T(8,128)S(1)} %bitcast_negate_fusion, f32[8,1,192,192]{3,2,1,0:T(8,128)S(1)} %bitcast.102, f32[8,1,192,192]{3,2,1,0:T(8,128)S(1)} %bitcast.101), kind=kLoop, calls=%fused_computation.14 | loop fusion | flops 1179648 | bytes 8257536 | tf_op jit(solution)/shard_map/stack | solution.py:36
  138.9 6.4 %convolution_bitcast_fusion = f32[8,1,2,36864]{3,0,2,1:T(8,128)} fusion(f32[1,2,8,36864]{3,1,0,2:T(2,128)} %all-gather.2.cloned.1.call-done, f32[8,1,2,8]{3,0,2,1:T(8,128)S(1)} %get-tuple-element.17, f32[8,1,2,8]{3,0,2,1:T(8,128)S(1)} %get-tuple-element.16), kind=kOutput, calls=%fused_computation | convolution fusion | flops 113246464 | bytes 4719616 | tf_op jit(solution)/shard_map/kuir,nirx->knux/dot_general | solution.py:81
  145.3 2.9 %reshape.272 = f32[8,2,192,192]{3,2,0,1:T(8,128)S(1)} reshape(f32[8,1,2,36864]{3,0,2,1:T(8,128)} %convolution_bitcast_fusion) | data formatting | bytes 4718592 | tf_op jit(solution)/shard_map/reshape.7
  148.3 8.1 %fusion.2 = f32[8,2,192,192,1]{3,2,4,1,0:T(8,128)S(1)} fusion(f32[8,1,2,192,192]{3,4,2,1,0:T(8,128)} %get-tuple-element.12, f32[8,1,2,192,192]{3,4,2,1,0:T(8,128)} %get-tuple-element.11, f32[8,2,192,192]{3,2,0,1:T(8,128)S(1)} %reshape.272), kind=kOutput, calls=%fused_computation.4 | convolution fusion | flops 2719088640 | bytes 9437184 | tf_op jit(solution)/shard_map/knibc,koicm->knobm/dot_general | solution.py:43
  156.4 6.0 %fusion.14 = f32[8,1,2,192,192]{3,4,2,0,1:T(8,128)S(1)} fusion(f32[8,1,2,192,192]{4,3,2,1,0:T(8,128)S(1)} %copy-done.1, f32[8,1,2,192,192]{4,3,2,1,0:T(8,128)S(1)} %copy-done, f32[8,2,192,192,1]{3,2,4,1,0:T(8,128)S(1)} %fusion.2), kind=kOutput, calls=%fused_computation.20 | convolution fusion | flops 2719088640 | bytes 9437184 | tf_op jit(solution)/shard_map/kojbp,knjbm->knopm/dot_general | solution.py:46
  163.3 2.5 %div.11 = f32[8,1,36864]{2,1,0:T(1,128)} reshape(f32[8,1,1,192,192]{4,3,0,2,1:T(8,128)S(1)} %copy.61) | data formatting | bytes 2359296 | tf_op jit(solution)/shard_map/div | solution.py:49
  (32 shorter events, 2.8 us)
Async XLA Ops:
  6.5 67.3 %all-reduce.3.cloned.1.call-start = ((), (), s32[]{:S(2)}) async-start(), calls=%async_computation.1 | async-start | bytes 2359296
  36.8 2.1 %copy-start.7 = (u32[32]{0:T(128)S(1)}, u32[32]{0:T(128)}, u32[]{:S(2)}) copy-start(u32[32]{0:T(128)} %constant.37) | copy-start | bytes 388
  36.8 39.4 %copy-start.4 = (s32[1,6]{1,0:T(1,128)S(1)}, s32[1,6]{1,0:T(1,128)}, u32[]{:S(2)}) copy-start(s32[1,6]{1,0:T(1,128)} %param.13) | copy-start | bytes 76
  36.8 39.4 %copy-start.6 = (s32[3]{0:T(128)S(1)}, s32[3]{0:T(128)}, u32[]{:S(2)}) copy-start(s32[3]{0:T(128)} %param.14) | copy-start | bytes 40
  36.8 61.8 %copy-start.3 = (f32[8,2,36864]{2,1,0:T(2,128)S(1)}, f32[8,2,36864]{2,1,0:T(2,128)}, u32[]{:S(2)}) copy-start(f32[8,2,36864]{2,1,0:T(2,128)} %param.17) | copy-start | bytes 7077892
  38.8 100.1 %all-gather.2.cloned.1.call-start = ((), (), s32[]{:S(2)}) async-start(), calls=%async_computation | async-start | bytes 2654208 | tf_op jit(solution)/shard_map/all_gather | solution.py:78
  122.7 5.5 %copy-start.5 = (s32[8,3]{0,1:T(4,128)S(1)}, s32[8,3]{0,1:T(4,128)}, u32[]{:S(2)}) copy-start(s32[8,3]{0,1:T(4,128)} %param.15) | copy-start | bytes 292
  134.0 1.4 copy-start.2
  148.2 8.1 %copy-start = (f32[8,1,2,192,192]{4,3,2,1,0:T(8,128)S(1)}, f32[8,1,2,192,192]{4,3,2,1,0:T(8,128)}, u32[]{:S(2)}) copy-start(f32[8,1,2,192,192]{4,3,2,1,0:T(8,128)} %get-tuple-element.13) | copy-start | bytes 7077892
  148.3 8.1 %copy-start.1 = (f32[8,1,2,192,192]{4,3,2,1,0:T(8,128)S(1)}, f32[8,1,2,192,192]{4,3,2,1,0:T(8,128)}, u32[]{:S(2)}) copy-start(f32[8,1,2,192,192]{4,3,2,1,0:T(8,128)} %get-tuple-element.14) | copy-start | bytes 7077892
Sparse Core Ops, SparseCore 0:
  38.9 34.8 all-reduce.2
  76.3 51.9 all-gather.1
where the time goes:
time: 176 us; the launch traced here: 173 us
  blocking collectives  44.1 us (25%)
  local copies, waits for them, and re-layouts  40.4 us (23%)
  waiting for transfers between devices  34.3 us (19%)
  matrix products  26.4 us (15%)
  between operations  15.1 us (9%)
  other arithmetic  12.4 us (7%)
    unnamed x3, waiting for transfers between devices  34.3 us
    psum x1, blocking collectives, broadcast(): return lax.psum(jnp.where(mine, shard, jnp.zeros_like(shard)), axis)  23.1 us
    all_gather x1, blocking collectives, body(): shard_geometry = lax.all_gather(geometry, 'row', axis=2, tiled=True)  21 us
    slice x2, local copies, waits for them, and re-layouts, complex_block(): imag_part = vectors[:, 1].reshape(pair_count, branches, branches)  17.6 us
    another operation x2, other arithmetic, complex_block(): return jnp.stack([upper_row, lower_row], axis=1)  9.22 us
    dot_general x1, matrix products, strengths(): jnp.einsum('knibc,koicm->knobm', shaped, complex_block(second_vectors, br...  8.11 us
    another operation x3, local copies, waits for them, and re-layouts, complex_block(): upper_row = jnp.stack([real_part, -imag_part], axis=1)  6.97 us
    dot_general x1, matrix products, body(): jnp.einsum('kuir,nirx->knux', rotation, shard_block, precision=HIGHEST)  6.41 us
  transfers between devices with their start and end apart: 2, of which 1 were waited for; matrix products, arithmetic and copies ran while one was open for 24% of the time, Pallas kernels for 0%

commit v1 on v0

--- a/solution.py
+++ b/solution.py
@@ -12,7 +12,7 @@
 
 def broadcast(shard, axis, root):
     mine = lax.axis_index(axis) == root
-    return lax.psum(jnp.where(mine, shard, jnp.zeros_like(shard)), axis)
+    return jnp.sum(lax.all_gather(jnp.where(mine, shard, jnp.zeros_like(shard)), axis), axis=0)
 
 
 def rotation_table(pair_rows, shift_rows, grid_size):

time: 176 us -> 189 us (1.074)
  blocking collectives: 44.1 us -> 53.4 us
  waiting for transfers between devices: 34.3 us -> 38 us
    all_gather x0 -> x1, blocking collectives: none -> 32.4 us  [broadcast(): lax.all_gather(jnp.where(mine, shard, jnp.zeros_like(shard)), axis)]
    psum x1 -> x0, blocking collectives: 23.1 us -> none  [broadcast(): return lax.psum(jnp.where(mine, shard, jnp.zeros_like(shard)), axis)]
    unnamed x3, waiting for transfers between devices: 34.3 us -> 38 us
  transfers between devices with their start and end apart: 2 -> 2, of which waited for: 1 -> 1; matrix products, arithmetic and copies ran while one was open for 24% -> 22% of each run, Pallas kernels for 0% -> 0%
where the time goes in v1:
time: 189 us; the launch traced here: 186 us
  blocking collectives  53.4 us (28%)
  local copies, waits for them, and re-layouts  40.4 us (21%)
  waiting for transfers between devices  38 us (20%)
  matrix products  26.4 us (14%)
  between operations  15.2 us (8%)
  other arithmetic  12.4 us (7%)
    unnamed x3, waiting for transfers between devices  38 us
    all_gather x1, blocking collectives, broadcast(): lax.all_gather(jnp.where(mine, shard, jnp.zeros_like(shard)), axis)  32.4 us
    all_gather x1, blocking collectives, body(): shard_geometry = lax.all_gather(geometry, 'row', axis=2, tiled=True)  21 us
    slice x2, local copies, waits for them, and re-layouts, complex_block(): imag_part = vectors[:, 1].reshape(pair_count, branches, branches)  17.6 us
    another operation x2, other arithmetic, complex_block(): return jnp.stack([upper_row, lower_row], axis=1)  9.22 us
    dot_general x1, matrix products, strengths(): jnp.einsum('knibc,koicm->knobm', shaped, complex_block(second_vectors, br...  8.12 us
    another operation x3, local copies, waits for them, and re-layouts, complex_block(): upper_row = jnp.stack([real_part, -imag_part], axis=1)  6.97 us
    dot_general x1, matrix products, body(): jnp.einsum('kuir,nirx->knux', rotation, shard_block, precision=HIGHEST)  6.41 us
  transfers between devices with their start and end apart: 2, of which 1 were waited for; matrix products, arithmetic and copies ran while one was open for 22% of the time, Pallas kernels for 0%

profile of v1, /device:TPU:0, one launch (start us, length us, event | category | flops | bytes accessed | tf_op | source)
XLA Modules:
  0.0 185.8 jit_solution(1240191346356299454)
XLA Ops:
  7.2 32.4 %all_gather.10 = f32[8,2,48,4]{2,3,1,0:T(4,128)S(1)} all-gather(f32[1,2,48,4]{2,3,1,0:T(4,128)S(1)} %broadcast_select_fusion), channel_id=1, replica_groups=mesh['row'=8,'ba'=4] {'row'}, dimensions={0}, use_global_device_ids=true | all-gather | bytes 13824 | tf_op jit(solution)/shard_map/all_gather | solution.py:15
  40.3 5.8 %fusion = f32[4,2,1,36864]{3,0,1,2:T(4,128)S(1)} fusion(f32[2,48,4]{1,2,0:T(4,128)S(1)} %reduce_sum.29, f32[1,48,36864]{2,1,0:T(8,128)} %param.9, f32[]{:T(128)} %bitcast.5), kind=kOutput, calls=%fused_computation.2 | convolution fusion | flops 170164224 | bytes 8259076 | tf_op jit(solution)/shard_map/san,rax->nsrx/dot_general | solution.py:69
  46.2 1.9 %copy.51 = f32[4,2,1,36864]{3,1,2,0:T(2,128)} copy(f32[4,2,1,36864]{3,0,1,2:T(4,128)S(1)} %fusion) | data formatting | bytes 2359296 | tf_op jit(solution)/shard_map/mul | solution.py:71
  48.8 37.9 %all-reduce.3.cloned.1.call-done = f32[4,2,1,36864]{3,1,2,0:T(2,128)} async-done(((f32[4,2,1,36864]{3,1,2,0:T(2,128)}), f32[4,2,1,36864]{3,1,2,0:T(2,128)}) %all-reduce.3.cloned.1.call-update) | async-done | bytes 1179664
  86.8 2.3 %dynamic-slice_bitcast_fusion = f32[1,2,1,36864]{3,1,0,2:T(2,128)} fusion(f32[4,2,1,36864]{3,1,2,0:T(2,128)} %all-reduce.3.cloned.1.call-done, u32[]{:T(128)} %bitcast.45), kind=kLoop, calls=%fused_computation.29 | loop fusion | bytes 589828 | tf_op jit(solution)/shard_map/reduce_scatter | solution.py:70
  89.1 0.7 subtract_bitcast_fusion
  89.8 0.7 fusion.29
  90.6 21.0 %all_gather.12 = f32[1,4,8]{1,0,2:T(1,128)S(1)} all-gather(f32[1,4,1]{1,0,2:T(1,128)S(1)} %fusion.29), channel_id=1, replica_groups=mesh['row'=8,'ba'=4] {'row'}, dimensions={2}, use_global_device_ids=true | all-gather | bytes 144 | tf_op jit(solution)/shard_map/all_gather | solution.py:79
  111.6 7.2 %slice_reduce_fusion.2 = (f32[8,36864]{1,0:T(8,128)S(1)}, f32[8,36864]{1,0:T(8,128)}) fusion(f32[8,2,36864]{2,1,0:T(2,128)S(1)} %copy-done.3), kind=kLoop, calls=%fused_computation.27 | loop fusion | bytes 4718592 | tf_op jit(solution)/shard_map/slice | solution.py:33
  118.8 0.7 reshape_squeeze.6
  120.1 1.3 neg.30
  121.4 2.0 %stack_reshape_squeeze.4 = f32[8,1,192,192]{3,2,0,1:T(8,128)S(1)} reshape(f32[8,36864]{1,0:T(8,128)} %get-tuple-element.6) | data formatting | bytes 2359296 | tf_op jit(solution)/shard_map/stack;reshape;squeeze | solution.py:34
  123.4 1.8 copy.48
  125.2 10.4 %slice_reduce_fusion = (f32[8,36864]{1,0:T(8,128)}, f32[8,36864]{1,0:T(8,128)}) fusion(f32[8,2,36864]{2,1,0:T(2,128)} %param.16), kind=kLoop, calls=%fused_computation.25 | loop fusion | bytes 4718592 | tf_op jit(solution)/shard_map/slice | solution.py:33
  135.6 2.0 %reshape_squeeze.7 = f32[8,1,192,192]{3,2,0,1:T(8,128)S(1)} reshape(f32[8,36864]{1,0:T(8,128)} %get-tuple-element.7) | data formatting | bytes 2359296 | tf_op jit(solution)/shard_map/reshape;squeeze | solution.py:33
  137.6 3.2 %stack_reshape_squeeze.5 = f32[8,1,192,192]{3,2,0,1:T(8,128)} reshape(f32[8,36864]{1,0:T(8,128)} %get-tuple-element.8) | data formatting | bytes 2359296 | tf_op jit(solution)/shard_map/stack;reshape;squeeze | solution.py:34
  141.2 5.7 %maximum_bitcast_fusion = (f32[8,1,2,192,192]{3,4,2,1,0:T(8,128)}, f32[8,1,2,192,192]{3,4,2,1,0:T(8,128)}) fusion(f32[8,1,192,192]{2,3,1,0:T(8,128)} %neg.30, f32[8,1,192,192]{2,3,1,0:T(8,128)} %copy.48, f32[8,1,192,192]{2,3,1,0:T(8,128)S(1)} %copy.47), kind=kLoop, calls=%fused_computation.12 | loop fusion | flops 1179648 | bytes 8257536 | tf_op jit(solution)/shard_map/stack | solution.py:36
  147.1 1.3 copy-done.2
  148.3 3.5 %maximum_bitcast_fusion.2 = (f32[8,1,2,192,192]{4,3,2,1,0:T(8,128)}, f32[8,1,2,192,192]{4,3,2,1,0:T(8,128)}) fusion(f32[8,1,192,192]{3,2,1,0:T(8,128)S(1)} %bitcast_negate_fusion, f32[8,1,192,192]{3,2,1,0:T(8,128)S(1)} %bitcast.100, f32[8,1,192,192]{3,2,1,0:T(8,128)S(1)} %bitcast.99), kind=kLoop, calls=%fused_computation.14 | loop fusion | flops 1179648 | bytes 8257536 | tf_op jit(solution)/shard_map/stack | solution.py:36
  151.9 6.4 %convolution_bitcast_fusion = f32[8,1,2,36864]{3,0,2,1:T(8,128)} fusion(f32[1,2,8,36864]{3,1,0,2:T(2,128)} %all-gather.2.cloned.1.call-done, f32[8,1,2,8]{3,0,2,1:T(8,128)S(1)} %get-tuple-element.17, f32[8,1,2,8]{3,0,2,1:T(8,128)S(1)} %get-tuple-element.16), kind=kOutput, calls=%fused_computation | convolution fusion | flops 113246464 | bytes 4719616 | tf_op jit(solution)/shard_map/kuir,nirx->knux/dot_general | solution.py:81
  158.3 2.9 %reshape.269 = f32[8,2,192,192]{3,2,0,1:T(8,128)S(1)} reshape(f32[8,1,2,36864]{3,0,2,1:T(8,128)} %convolution_bitcast_fusion) | data formatting | bytes 4718592 | tf_op jit(solution)/shard_map/reshape.7
  161.2 8.1 %fusion.2 = f32[8,2,192,192,1]{3,2,4,1,0:T(8,128)S(1)} fusion(f32[8,1,2,192,192]{3,4,2,1,0:T(8,128)} %get-tuple-element.12, f32[8,1,2,192,192]{3,4,2,1,0:T(8,128)} %get-tuple-element.11, f32[8,2,192,192]{3,2,0,1:T(8,128)S(1)} %reshape.269), kind=kOutput, calls=%fused_computation.4 | convolution fusion | flops 2719088640 | bytes 9437184 | tf_op jit(solution)/shard_map/knibc,koicm->knobm/dot_general | solution.py:43
  169.4 6.0 %fusion.14 = f32[8,1,2,192,192]{3,4,2,0,1:T(8,128)S(1)} fusion(f32[8,1,2,192,192]{4,3,2,1,0:T(8,128)S(1)} %copy-done.1, f32[8,1,2,192,192]{4,3,2,1,0:T(8,128)S(1)} %copy-done, f32[8,2,192,192,1]{3,2,4,1,0:T(8,128)S(1)} %fusion.2), kind=kOutput, calls=%fused_computation.20 | convolution fusion | flops 2719088640 | bytes 9437184 | tf_op jit(solution)/shard_map/kojbp,knjbm->knopm/dot_general | solution.py:46
  176.2 2.5 %div.11 = f32[8,1,36864]{2,1,0:T(1,128)} reshape(f32[8,1,1,192,192]{4,3,0,2,1:T(8,128)S(1)} %copy.61) | data formatting | bytes 2359296 | tf_op jit(solution)/shard_map/div | solution.py:49
  (33 shorter events, 2.8 us)
Async XLA Ops:
  6.5 80.2 %all-reduce.3.cloned.1.call-start = ((), (), s32[]{:S(2)}) async-start(), calls=%async_computation.1 | async-start | bytes 2359296
  46.1 2.1 %copy-start.7 = (u32[32]{0:T(128)S(1)}, u32[32]{0:T(128)}, u32[]{:S(2)}) copy-start(u32[32]{0:T(128)} %constant.38) | copy-start | bytes 388
  46.1 43.0 %copy-start.4 = (s32[1,6]{1,0:T(1,128)S(1)}, s32[1,6]{1,0:T(1,128)}, u32[]{:S(2)}) copy-start(s32[1,6]{1,0:T(1,128)} %param.13) | copy-start | bytes 76
  46.1 43.0 %copy-start.6 = (s32[3]{0:T(128)S(1)}, s32[3]{0:T(128)}, u32[]{:S(2)}) copy-start(s32[3]{0:T(128)} %param.14) | copy-start | bytes 40
  46.2 65.5 %copy-start.3 = (f32[8,2,36864]{2,1,0:T(2,128)S(1)}, f32[8,2,36864]{2,1,0:T(2,128)}, u32[]{:S(2)}) copy-start(f32[8,2,36864]{2,1,0:T(2,128)} %param.17) | copy-start | bytes 7077892
  48.1 103.7 %all-gather.2.cloned.1.call-start = ((), (), s32[]{:S(2)}) async-start(), calls=%async_computation | async-start | bytes 2654208 | tf_op jit(solution)/shard_map/all_gather | solution.py:78
  135.6 5.5 %copy-start.5 = (s32[8,3]{0,1:T(4,128)S(1)}, s32[8,3]{0,1:T(4,128)}, u32[]{:S(2)}) copy-start(s32[8,3]{0,1:T(4,128)} %param.15) | copy-start | bytes 292
  146.9 1.4 copy-start.2
  161.2 8.1 %copy-start = (f32[8,1,2,192,192]{4,3,2,1,0:T(8,128)S(1)}, f32[8,1,2,192,192]{4,3,2,1,0:T(8,128)}, u32[]{:S(2)}) copy-start(f32[8,1,2,192,192]{4,3,2,1,0:T(8,128)} %get-tuple-element.13) | copy-start | bytes 7077892
  161.2 8.1 %copy-start.1 = (f32[8,1,2,192,192]{4,3,2,1,0:T(8,128)S(1)}, f32[8,1,2,192,192]{4,3,2,1,0:T(8,128)}, u32[]{:S(2)}) copy-start(f32[8,1,2,192,192]{4,3,2,1,0:T(8,128)} %get-tuple-element.14) | copy-start | bytes 7077892
Sparse Core Ops, SparseCore 0:
  48.2 38.4 all-reduce.2
  89.2 51.9 all-gather.1
